TPU v7x, 256 devices: a whole 4x4x8 slice. The times are simulated.
256 devices in a mesh: row: 16 (over z_lo, x, core), col: 4 (over y), item: 4 (over z_hi).
Axes of the slice: x: 4, y: 4, z: 8 (z_hi: 4, z_lo: 2; z = z_hi * 2 + z_lo), core: 2. Of those that a mesh axis runs over, the one named last changes fastest.
Arguments:
- tokens: bfloat16 [4, 16, 64, 2432], P('item', 'row', 'col'), may hold values from -6 to 6
- text_keys_values: bfloat16 [4, 154, 2, 2048], P('item', None, None, 'row'), may hold values from -200 to 200
- text_length: int32 [4], P('item'), may hold values from 2 to 154, as said below
- modulation: float32 [4, 8, 2432], P('item'), may hold values from -4 to 4
- input_weight: bfloat16 [2432, 3, 2048], P(None, None, 'row'), may hold values from -0.125 to 0.125
- norm_gain: float32 [2, 64], replicated, may hold values from 1 to 3
- output_weight: bfloat16 [2048, 2432], P('row'), may hold values from -0.125 to 0.125
- up_weight: bfloat16 [2432, 9728], P(None, 'row'), may hold values from -0.125 to 0.125
- down_weight: bfloat16 [9728, 2432], P('row'), may hold values from -0.0625 to 0.0625
- final_weight: bfloat16 [2432, 64], replicated, may hold values from -0.125 to 0.125
- step_index: int32 [1], replicated, may hold values from 0 to 27
- latent: float32 [4, 16, 4096], P('item', 'row', 'col'), may hold values from -6 to 6
Outputs:
- tokens_out: bfloat16 [4, 16, 64, 2432], P('item', 'row', 'col')
- velocity: float32 [4, 16, 4096], P('item', 'row', 'col')
- latent_next: float32 [4, 16, 4096], P('item', 'row', 'col')
Inputs may be any that keep to these rules, and one draw needn't show every extreme that they name: `text_length`: at least one sequence has all 154 text tokens valid.
All inputs are finite; a program needn't handle non-finite values.
Results may differ from a plain program's by a relative error of at most 0.024.
Values may be sent and summed in bfloat16 or wider, within the bound.
A program may use at most 64 MiB of HBM per device.

v0:
```python
import jax
import jax.numpy as jnp
from jax import lax
from jax.sharding import PartitionSpec as P

HD = 64
STEPS = 28


EPSILON = 1e-06
SHIFT_FACTOR = 3.0
GUIDANCE = 4.5
MASKED = -1e30


def partner_2(value, axis, apart):
    mask = 2**apart
    pairs = [(source, source ^ mask) for source in range(lax.axis_size(axis))]
    return lax.ppermute(value, axis, pairs)


def layer_norm(values):
    center = values - jnp.mean(values, axis=-1, keepdims=True)
    spread = jnp.mean(center * center, axis=-1, keepdims=True)
    return center * lax.rsqrt(spread + EPSILON)


def modulate(values, shift_term, scale_term):
    return (layer_norm(values) * (1.0 + scale_term) + shift_term).astype(jnp.bfloat16)


def root_norm(values, gain_row):
    return (
        values * lax.rsqrt(jnp.mean(values * values, axis=-1, keepdims=True) + EPSILON) * gain_row
    )


def noise_level(position):
    linear = 1.0 - position / STEPS
    return SHIFT_FACTOR * linear / (1.0 + (SHIFT_FACTOR - 1.0) * linear)


def on_device(
    tokens,
    text_keys_values,
    text_length,
    modulation,
    input_weight,
    norm_gain,
    output_weight,
    up_weight,
    down_weight,
    final_weight,
    step_index,
    latent,
):
    tile_rows = tokens.shape[1] * tokens.shape[2]
    model_width = tokens.shape[3]
    mod_rows = modulation[0]
    row_position = lax.axis_index("row")
    stripe_tokens = lax.all_gather(tokens, "row", axis=1, tiled=True)
    stripe_states = stripe_tokens.reshape(-1, model_width).astype(jnp.float32)
    stripe_rows = stripe_states.shape[0]
    local_width = input_weight.shape[2]
    local_heads = local_width // HD
    attn_input = modulate(stripe_states, mod_rows[0], mod_rows[1])
    projected = jnp.dot(
        attn_input,
        input_weight.reshape(model_width, 3 * local_width),
        preferred_element_type=jnp.float32,
    )
    projected = projected.reshape(stripe_rows, 3, local_heads, HD)
    queries = root_norm(projected[:, 0], norm_gain[0]).astype(jnp.bfloat16).transpose(1, 0, 2)
    keys_image = (
        root_norm(projected[:, 1], norm_gain[1])
        .astype(jnp.bfloat16)
        .reshape(stripe_rows, local_width)
    )
    values_image = projected[:, 2].astype(jnp.bfloat16).reshape(stripe_rows, local_width)
    text_pairs = text_keys_values[0]
    keys_text = text_pairs[:, 0].reshape(-1, local_heads, HD)
    values_text = text_pairs[:, 1].reshape(-1, local_heads, HD)
    text_valid = jnp.arange(keys_text.shape[0]) < text_length[0]
    text_scores = jnp.einsum(
        "hsd,thd->hst", queries, keys_text, preferred_element_type=jnp.float32
    ) * HD ** (-0.5)
    text_scores = jnp.where(text_valid[None, None, :], text_scores, MASKED)
    largest = jnp.max(text_scores, axis=-1)
    text_weights = jnp.exp(text_scores - largest[..., None])
    total_mass = jnp.sum(text_weights, axis=-1)
    weighted = jnp.einsum(
        "hst,thd->hsd",
        text_weights.astype(jnp.bfloat16),
        values_text,
        preferred_element_type=jnp.float32,
    )

    def one_block(running, block_pair):
        running_max, running_mass, running_sum = running
        key_block, value_block = block_pair
        scores = jnp.einsum(
            "hsd,khd->hsk", queries, key_block, preferred_element_type=jnp.float32
        ) * HD ** (-0.5)
        new_max = jnp.maximum(running_max, jnp.max(scores, axis=-1))
        factor = jnp.exp(running_max - new_max)
        weights = jnp.exp(scores - new_max[..., None])
        new_mass = running_mass * factor + jnp.sum(weights, axis=-1)
        new_sum = running_sum * factor[..., None] + jnp.einsum(
            "hsk,khd->hsd",
            weights.astype(jnp.bfloat16),
            value_block,
            preferred_element_type=jnp.float32,
        )
        return ((new_max, new_mass, new_sum), None)

    key_piece = lax.all_gather(keys_image, "col", axis=0, tiled=True)
    value_piece = lax.all_gather(values_image, "col", axis=0, tiled=True)
    blocks = key_piece.shape[0] // stripe_rows
    key_blocks = key_piece.reshape(blocks, stripe_rows, local_heads, HD)
    value_blocks = value_piece.reshape(blocks, stripe_rows, local_heads, HD)
    result, unused = lax.scan(
        one_block, (largest, total_mass, weighted), (key_blocks, value_blocks)
    )
    largest, total_mass, weighted = result
    attended = (
        (weighted / total_mass[..., None])
        .astype(jnp.bfloat16)
        .transpose(1, 0, 2)
        .reshape(stripe_rows, local_width)
    )
    attention = lax.psum(
        jnp.dot(attended, output_weight, preferred_element_type=jnp.float32).astype(jnp.bfloat16),
        "row",
    ).astype(jnp.float32)
    stripe_middle = stripe_states + mod_rows[2] * attention
    feed_input = modulate(stripe_middle, mod_rows[3], mod_rows[4])
    hidden = jax.nn.gelu(
        jnp.dot(feed_input, up_weight, preferred_element_type=jnp.float32), approximate=True
    ).astype(jnp.bfloat16)
    middle = lax.dynamic_slice_in_dim(stripe_middle, row_position * tile_rows, tile_rows, 0)
    feed = lax.psum_scatter(
        jnp.dot(hidden, down_weight, preferred_element_type=jnp.float32).astype(jnp.bfloat16),
        "row",
        scatter_dimension=0,
        tiled=True,
    ).astype(jnp.float32)
    leaving = middle + mod_rows[5] * feed
    tokens_out = leaving.astype(jnp.bfloat16).reshape(tokens.shape)
    final_input = modulate(leaving, mod_rows[6], mod_rows[7])
    raw_velocity = jnp.dot(final_input, final_weight, preferred_element_type=jnp.float32).reshape(
        1, tokens.shape[1], -1
    )
    partner = partner_2(raw_velocity, "item", 0)
    is_guided = lax.axis_index("item") % 2 == 0
    guided = jnp.where(is_guided, raw_velocity, partner)
    unguided = jnp.where(is_guided, partner, raw_velocity)
    velocity = unguided + GUIDANCE * (guided - unguided)
    position = step_index[0].astype(jnp.float32)
    step_size = noise_level(position + 1.0) - noise_level(position)
    return (tokens_out, velocity, latent + step_size * velocity)


def solution(mesh):
    in_specs = (
        P("item", "row", "col", None),
        P("item", None, None, "row"),
        P("item"),
        P("item", None, None),
        P(None, None, "row"),
        P(),
        P("row", None),
        P(None, "row"),
        P("row", None),
        P(),
        P(),
        P("item", "row", "col"),
    )
    out_specs = (P("item", "row", "col", None), P("item", "row", "col"), P("item", "row", "col"))
    return jax.shard_map(
        on_device, mesh=mesh, in_specs=in_specs, out_specs=out_specs, check_vma=False
    )
```

profile of v0, /device:TPU:32, one launch (start us, length us, event | category | flops | bytes accessed | tf_op | source)
XLA Modules:
  0.0 310.3 jit_solution(12788335768457517483)
XLA Ops:
  7.3 0.7 all-gather.2.cloned.1.call-update
  8.0 4.1 %copy.26 = bf16[2432,3,128]{0,2,1:T(8,128)(2,1)} copy(bf16[2432,3,128]{2,0,1:T(8,128)(2,1)} %param.18) | data formatting | bytes 3735552 | tf_op args[4]
  13.2 0.7 add_reduce_fusion
  13.9 33.5 %all-gather.2.cloned.1.call-done = bf16[1,16,16,2432]{3,2,0,1:T(8,128)(2,1)} async-done(((bf16[1,1,16,2432]{3,2,0,1:T(8,128)(2,1)}), bf16[1,16,16,2432]{3,2,0,1:T(8,128)(2,1)}) %all-gather.2.cloned.1.call-update) | async-done | bytes 1245200 | tf_op jit(solution)/shard_map/all_gather | solution.py:61
  47.5 1.7 convert_reduce_fusion
  49.2 1.7 multiply_reduce_fusion.1
  50.9 0.6 add_convert_fusion.1
  51.5 0.7 fusion.55
  53.1 12.6 %all_gather.10 = bf16[1024,128]{0,1:T(8,128)(2,1)S(1)} all-gather(bf16[256,128]{0,1:T(8,128)(2,1)S(1)} %fusion.35), channel_id=1, replica_groups=mesh['row'=16,'col'=4,'item'=4] {'col'}, dimensions={0}, use_global_device_ids=true | all-gather | bytes 327680 | tf_op jit(solution)/shard_map/all_gather | solution.py:116
  65.7 0.9 reshape.190
  66.5 1.0 copy.29
  67.5 13.2 %all_gather.11 = bf16[1024,128]{0,1:T(8,128)(2,1)} all-gather(bf16[256,128]{0,1:T(8,128)(2,1)S(1)} %bitcast.82), channel_id=1, replica_groups=mesh['row'=16,'col'=4,'item'=4] {'col'}, dimensions={0}, use_global_device_ids=true | all-gather | bytes 327680 | tf_op jit(solution)/shard_map/all_gather | solution.py:117
  80.7 1.8 reshape.191
  82.6 1.7 copy.30
  84.2 6.1 %while.14 = (s32[]{:T(128)}, f32[2,256]{1,0:T(2,128)S(1)}, f32[2,256]{1,0:T(2,128)S(1)}, f32[2,256,64]{1,2,0:T(8,128)S(1)}, bf16[4,256,2,64]{1,3,2,0:T(8,128)(2,...) while((s32[]{:T(128)}, f32[2,256]{1,0:T(2,128)S(1)}, ...), condition=%wide.region_9.10_spmd, body=%wide.region_6.9_spmd.sunk | while | flops 34407424 | bytes 2064985 | solution.py:121
  84.7 1.1 convolution_add_fusion.2
  86.2 1.1 convolution_add_fusion.2
  87.7 1.1 convolution_add_fusion.2
  89.3 1.1 convolution_add_fusion.2
  90.4 2.7 convolution_convert_fusion
  93.1 124.5 %all-reduce.2.cloned.1.call-done = bf16[256,2432]{1,0:T(8,128)(2,1)} async-done(((bf16[256,2432]{1,0:T(8,128)(2,1)}), bf16[256,2432]{1,0:T(8,128)(2,1)}) %all-reduce.2.cloned.1.call-update) | async-done | bytes 1245200 | tf_op jit(solution)/shard_map/psum | solution.py:131
  217.6 2.2 fusion.51
  219.8 1.4 copy-done.2
  221.2 0.4 multiply_reduce_fusion
  221.7 7.5 %convolution_convert_fusion.1 = bf16[256,2432]{1,0:T(8,128)(2,1)} fusion(bf16[608,2432]{1,0:T(8,128)(2,1)S(1)} %copy-done, bf16[2432,608]{0,1:T(8,128)(2,1)} %param.21, f32[256,2432]{1,0:T(8,128)} %copy-done.2, f32[2432]{0:T(1024)S(1)} %get-tuple-element.58, f32[2432]{0:T(1024)S(1)} %copy-done.7, f32[256]{0:T(256)S(1)} %add_rsqrt_fusion.3, ...), kind=kOutput, calls=%fused_computation.16 | convolution fusion | flops 1519280128 | bytes 9671680 | tf_op jit(solution)/shard_map/dot_general | solution.py:142
  229.2 65.3 %reduce-scatter.2.cloned.1.call-done = bf16[16,2432]{1,0:T(8,128)(2,1)} async-done(((bf16[256,2432]{1,0:T(8,128)(2,1)}), bf16[16,2432]{1,0:T(8,128)(2,1)}) %reduce-scatter.2.cloned.1.call-update) | async-done | bytes 77840 | tf_op jit(solution)/shard_map/reduce_scatter | solution.py:141
  294.5 1.1 fusion.49
  295.6 1.7 multiply_reduce_fusion.2
  297.4 1.2 fusion.36
  298.7 2.4 collective-permute-start
  301.8 1.4 collective-permute-done
  303.2 0.6 multiply_add_fusion.2
  (69 shorter events, 3.2 us)
Async XLA Ops:
  7.2 214.5 %copy-start = (bf16[608,2432]{1,0:T(8,128)(2,1)S(1)}, bf16[608,2432]{1,0:T(8,128)(2,1)}, u32[]{:S(2)}) copy-start(bf16[608,2432]{1,0:T(8,128)(2,1)} %param.22) | copy-start | bytes 8871940
  7.2 4.9 %copy-start.4 = (bf16[1,154,2,128]{3,2,1,0:T(2,128)(2,1)S(1)}, bf16[1,154,2,128]{3,2,1,0:T(2,128)(2,1)}, u32[]{:S(2)}) copy-start(bf16[1,154,2,128]{3,2,1,0:T(2,128)(2,1)} %param.15) | copy-start | bytes 236548
  7.2 5.9 %copy-start.9 = (f32[2,64]{1,0:T(2,128)S(1)}, f32[2,64]{1,0:T(2,128)}, u32[]{:S(2)}) copy-start(f32[2,64]{1,0:T(2,128)} %param.19) | copy-start | bytes 1540
  7.2 6.0 %copy-start.6 = (f32[1,8,2432]{2,1,0:T(8,128)S(1)}, f32[1,8,2432]{2,1,0:T(8,128)}, u32[]{:S(2)}) copy-start(f32[1,8,2432]{2,1,0:T(8,128)} %param.17) | copy-start | bytes 233476
  7.2 40.3 %all-gather.2.cloned.1.call-start = ((), (), s32[]{:S(2)}) async-start(), calls=%async_computation.1 | async-start | bytes 1323008 | tf_op jit(solution)/shard_map/all_gather | solution.py:61
  7.9 209.7 %all-reduce.2.cloned.1.call-start = ((), (), s32[]{:S(2)}) async-start(), calls=%async_computation.2 | async-start | bytes 2490368 | tf_op jit(solution)/shard_map/psum | solution.py:131
  47.5 3.5 %copy-start.1 = (bf16[1,16,16,2432]{3,2,0,1:T(8,128)(2,1)S(1)}, bf16[1,16,16,2432]{3,2,0,1:T(8,128)(2,1)}, u32[]{:S(2)}) copy-start(bf16[1,16,16,2432]{3,2,0,1:T(8,128)(2,1)} %all-gather.2.cloned.1.call-done) | copy-start | bytes 3735556
  47.5 4.1 %copy-start.3 = (bf16[2432,3,128]{0,2,1:T(8,128)(2,1)S(1)}, bf16[2432,3,128]{0,2,1:T(8,128)(2,1)}, u32[]{:S(2)}) copy-start(bf16[2432,3,128]{0,2,1:T(8,128)(2,1)} %copy.26) | copy-start | bytes 5603332
  93.1 201.5 %reduce-scatter.2.cloned.1.call-start = ((), (), s32[]{:S(2)}) async-start(), calls=%async_computation.3 | async-start | bytes 1323008 | tf_op jit(solution)/shard_map/reduce_scatter | solution.py:141
  219.8 1.4 copy-start.2
  219.8 1.9 copy-start.7
  221.6 75.7 %copy-start.5 = (bf16[2432,64]{0,1:T(8,128)(2,1)S(1)}, bf16[2432,64]{0,1:T(8,128)(2,1)}, u32[]{:S(2)}) copy-start(bf16[2432,64]{0,1:T(8,128)(2,1)} %param.23) | copy-start | bytes 933892
  229.2 74.0 %copy-start.8 = (f32[1,1,1024]{2,1,0:T(1,128)S(1)}, f32[1,1,1024]{2,1,0:T(1,128)}, u32[]{:S(2)}) copy-start(f32[1,1,1024]{2,1,0:T(1,128)} %param.25) | copy-start | bytes 12292
  298.7 4.5 %collective-permute-start = (f32[1,1,1024]{2,1,0:T(1,128)S(1)}, f32[1,1,1024]{2,1,0:T(1,128)S(1)}, u32[]{:S(2)}, u32[]{:S(2)}) collective-permute-start(f32[1,1,1024]{2,1,0:T(1,128)S(1)} %reshape.194), channel_id=1, source_target_pairs={{0,1},{1,0},{2,3},{3,2},{4,5},{5,4},{6,7},{7,6},{8,9},{9,8},{10,11... | collective-permute-start | bytes 12296 | tf_op jit(solution)/shard_map/ppermute | solution.py:19
Sparse Core Ops, SparseCore 0:
  9.9 37.5 all-gather.1
  93.2 124.3 all-reduce.1
  229.3 65.1 reduce-scatter.1
where the time goes:
time: 312 us; the launch traced here: 310 us
  waiting for transfers between devices  225 us (72%)
  blocking collectives  25.8 us (8%)
  matrix products  18 us (6%)
  between operations  15.4 us (5%)
  local copies, waits for them, and re-layouts  11.5 us (4%)
  other arithmetic  11.5 us (4%)
    psum x1, waiting for transfers between devices, on_device(): lax.psum(jnp.dot(attended, output_weight, preferred_element_type=jnp.floa...  124 us
    reduce_scatter x1, waiting for transfers between devices, on_device(): lax.psum_scatter(jnp.dot(hidden, down_weight, preferred_element_type=jnp....  65.3 us
    all_gather x1, waiting for transfers between devices, on_device(): stripe_tokens = lax.all_gather(tokens, 'row', axis=1, tiled=True)  33.5 us
    all_gather x1, blocking collectives, on_device(): value_piece = lax.all_gather(values_image, 'col', axis=0, tiled=True)  13.2 us
    all_gather x1, blocking collectives, on_device(): key_piece = lax.all_gather(keys_image, 'col', axis=0, tiled=True)  12.6 us
    dot_general x1, matrix products, on_device(): jnp.dot(hidden, down_weight, preferred_element_type=jnp.float32)  7.51 us
  transfers between devices with their start and end apart: 4, of which 4 were waited for; matrix products, arithmetic and copies ran while one was open for 2% of the time, Pallas kernels for 0%

commit v1 on v0

v1 whole, which is shorter than its diff:
```python
import functools

import jax
import jax.numpy as jnp
from jax import lax
from jax.experimental import pallas as pl
from jax.experimental.pallas import tpu as pltpu
from jax.sharding import PartitionSpec as P

HD = 64
STEPS = 28
EPSILON = 1e-06
SHIFT_FACTOR = 3.0
GUIDANCE = 4.5
MASKED = -1e30
MESH = pl.DeviceIdType.MESH
BF16 = jnp.bfloat16
F32 = jnp.float32

PEERS = ((1, 2), (0, 2), (1, 1), (1, 3), (0, 1), (0, 3), (1, 0))
TEXT_PAD = 160


def slot_of(dz, dx):
    return (dz % 2) * 4 + dx % 4


def layer_norm(values):
    center = values - jnp.mean(values, axis=-1, keepdims=True)
    spread = jnp.mean(center * center, axis=-1, keepdims=True)
    return center * lax.rsqrt(spread + EPSILON)


def modulate(values, shift_term, scale_term):
    return (layer_norm(values) * (1.0 + scale_term) + shift_term).astype(BF16)


def noise_level(position):
    linear = 1.0 - position / STEPS
    return SHIFT_FACTOR * linear / (1.0 + (SHIFT_FACTOR - 1.0) * linear)


def nt_dot(left, right):
    return lax.dot_general(left, right, (((1,), (1,)), ((), ())), preferred_element_type=F32)


def layer_kernel(
    length_ref, step_ref, tok_hbm, text_hbm, mod_hbm, win_hbm, gain_hbm, wo_hbm, wu_hbm, wd_hbm, wf_hbm, lat_hbm,
    out_tok, out_vel, out_lat,
    tok, text, mod, wi, gain, wo, wu, wd, wf, lat,
    g1, g2, p1, p2, r1, r2, kvr, kvs, qb, qs, ab, ats, s_max, s_sum, s_acc, vraw, vx, vr,
    local_sem, w_send, w_recv, g1_send, g1_recv, kv_send, kv_recv, q_send, q_recv, a_send, a_recv,
    r1_send, r1_recv, g2_send, g2_recv, r2_send, r2_recv, v_send, v_recv,
):
    tile, width = tok.shape
    half = tile * 8
    ff = wu_hbm.shape[0]
    row = lax.axis_index("row")
    col = lax.axis_index("col")
    item = lax.axis_index("item")
    z, x, k = row // 8, (row // 2) % 4, row % 2

    def device(dz=0, dx=0, dk=0, dc=0, other_item=False):
        row_to = ((z + dz) % 2) * 8 + ((x + dx) % 4) * 2 + (k + dk) % 2
        item_to = item + 1 - 2 * (item % 2) if other_item else item
        return (row_to, (col + dc) % 4, item_to)

    def send(src, dst, send_sem, recv_sem, to):
        copy = pltpu.make_async_remote_copy(
            src_ref=src, dst_ref=dst, send_sem=send_sem, recv_sem=recv_sem, device_id=to, device_id_type=MESH
        )
        copy.start()
        return copy

    pairs = [(tok_hbm, tok), (mod_hbm, mod)]
    pairs += [(win_hbm.at[j], wi.at[:, pl.ds(128 * j, 128)]) for j in range(3)]
    pairs += [(text_hbm, text), (gain_hbm, gain), (wo_hbm, wo.at[pl.ds(0, 128)])]
    pairs += [(wu_hbm, wu.at[pl.ds(0, ff)]), (wd_hbm, wd.at[pl.ds(0, ff)]), (wf_hbm, wf), (lat_hbm, lat)]
    loads = [pltpu.make_async_copy(src, dst, local_sem.at[j]) for j, (src, dst) in enumerate(pairs)]
    for load in loads:
        load.start()

    friends = [device(dz, dx) for dz, dx in PEERS] + [device(dk=1), device(other_item=True)]
    friends += [device(dk=dk, dc=dc) for dc in (1, 2, 3) for dk in (0, 1)]
    barrier = pltpu.get_barrier_semaphore()
    for friend in friends:
        pl.semaphore_signal(barrier, inc=1, device_id=friend, device_id_type=MESH)

    loads[0].wait()
    loads[1].wait()
    states = tok[...].astype(F32)
    g1[pl.ds(0, tile), :] = modulate(states, mod[0:1, :], mod[1:2, :])
    pl.semaphore_wait(barrier, len(friends))

    def spread(buf, send_sems, recv_sems):
        copies = []
        for n, (dz, dx) in enumerate(PEERS):
            to = slot_of(dz, -dx)
            copies.append(
                send(
                    buf.at[pl.ds(0, tile)], buf.at[pl.ds(to * tile, tile)], send_sems.at[n], recv_sems.at[n],
                    device(dz, dx),
                )
            )
        return copies

    gather1 = spread(g1, g1_send, g1_recv)
    sibling = device(dk=1)
    weight_pairs = [(win_hbm.at[j], wi.at[:, pl.ds(384 + 128 * j, 128)]) for j in range(3)]
    weight_pairs += [(wo_hbm, wo.at[pl.ds(128, 128)]), (wu_hbm, wu.at[pl.ds(ff, ff)]), (wd_hbm, wd.at[pl.ds(ff, ff)])]
    shared = [send(src, dst, w_send.at[j], w_recv.at[j], sibling) for j, (src, dst) in enumerate(weight_pairs)]

    loads[5].wait()
    loads[6].wait()
    text_rows = text.shape[0]
    picked = lax.broadcasted_iota(jnp.int32, (TEXT_PAD, text_rows), 1)
    wanted = 2 * lax.broadcasted_iota(jnp.int32, (TEXT_PAD, text_rows), 0)
    text_all = text[...]
    key_text = jnp.dot((picked == wanted).astype(BF16), text_all, preferred_element_type=F32).astype(BF16)
    value_text = jnp.dot((picked == wanted + 1).astype(BF16), text_all, preferred_element_type=F32).astype(BF16)
    gains = gain[...]
    gain_rows = jnp.concatenate([gains, gains], axis=1)
    lane = lax.broadcasted_iota(jnp.int32, (1, 128), 1)
    head_masks = ((lane < HD).astype(BF16), (lane >= HD).astype(BF16))

    def root_norm(values, gain_row):
        squares = values * values
        first = jnp.sum(jnp.where(lane < HD, squares, 0.0), axis=1, keepdims=True)
        second = jnp.sum(jnp.where(lane < HD, 0.0, squares), axis=1, keepdims=True)
        mean = jnp.where(lane < HD, first, second) * (1.0 / HD)
        return values * lax.rsqrt(mean + EPSILON) * gain_row

    for j in (2, 3, 4):
        loads[j].wait()
    for copy in shared[:3]:
        copy.wait()
    for copy in gather1:
        copy.wait()
    projected = jnp.dot(g1[...], wi[...], preferred_element_type=F32)

    kvs[:, 0:128] = root_norm(projected[:, 512:640], gain_rows[1:2]).astype(BF16)
    kvs[:, 128:256] = projected[:, 640:768].astype(BF16)
    kvr[0, 0, :, 0:128] = root_norm(projected[:, 128:256], gain_rows[1:2]).astype(BF16)
    kvr[0, 0, :, 128:256] = projected[:, 256:384].astype(BF16)
    kv_copies = {}
    for dc in (2, 1, 3):
        kv_copies[4 - dc] = [
            send(kvr.at[0, 0], kvr.at[4 - dc, 0], kv_send.at[dc, 0], kv_recv.at[4 - dc, 0], device(dc=dc)),
            send(kvs, kvr.at[4 - dc, 1], kv_send.at[dc, 1], kv_recv.at[4 - dc, 1], device(dk=1, dc=dc)),
        ]
    own_pair = send(kvs, kvr.at[0, 1], kv_send.at[0, 1], kv_recv.at[0, 1], sibling)
    qs[...] = (root_norm(projected[:, 384:512], gain_rows[0:1]) * HD ** (-0.5)).astype(BF16)
    q_copy = send(qs, qb.at[pl.ds(half, half)], q_send, q_recv, sibling)
    qb[pl.ds(0, half), :] = (root_norm(projected[:, 0:128], gain_rows[0:1]) * HD ** (-0.5)).astype(BF16)

    def attend(keys, values, chunks, keep=None):
        for n in chunks:
            rows = pl.ds(n * half, half)
            query = qb[pl.ds((n % 2) * half, half), :] * head_masks[n // 2]
            scores = nt_dot(query, keys)
            if keep is not None:
                scores = jnp.where(keep, scores, MASKED)
            old = s_max[rows, :]
            new = jnp.maximum(old, jnp.max(scores, axis=1, keepdims=True))
            factor = jnp.exp(old - new)
            weights = jnp.exp(scores - new[:, 0:1])
            s_max[rows, :] = new
            s_sum[rows, :] = s_sum[rows, :] * factor + jnp.sum(weights, axis=1, keepdims=True)
            s_acc[rows, :] = s_acc[rows, :] * factor + jnp.dot(
                weights.astype(BF16), values, preferred_element_type=F32
            )

    s_max[...] = jnp.full_like(s_max, MASKED)
    s_sum[...] = jnp.zeros_like(s_sum)
    s_acc[...] = jnp.zeros_like(s_acc)
    keep = lax.broadcasted_iota(jnp.int32, (1, TEXT_PAD), 1) < length_ref[0]
    attend(kvr[0, 0, :, 0:128], kvr[0, 0, :, 128:256], (0, 2))
    attend(key_text, value_text, (0, 2), keep)
    q_copy.wait()
    own_pair.wait()
    attend(kvr[0, 0, :, 0:128], kvr[0, 0, :, 128:256], (1, 3))
    attend(key_text, value_text, (1, 3), keep)
    attend(kvr[0, 1, :, 0:128], kvr[0, 1, :, 128:256], (1, 3, 0, 2))
    for dc in (1, 3, 2):
        for copy in kv_copies[dc]:
            copy.wait()
        for part in range(2):
            attend(kvr[dc, part, :, 0:128], kvr[dc, part, :, 128:256], (1, 3, 0, 2))

    def attended(parity):
        low, high = pl.ds(parity * half, half), pl.ds((2 + parity) * half, half)
        first = s_acc[low, :] / s_sum[low, :]
        second = s_acc[high, :] / s_sum[high, :]
        return jnp.where(lane < HD, first, second).astype(BF16)

    ats[...] = attended(1)
    a_copy = send(ats, ab.at[:, pl.ds(128, 128)], a_send, a_recv, sibling)
    ab[:, 0:128] = attended(0)
    loads[7].wait()
    shared[3].wait()
    a_copy.wait()

    columns = [(n, min(512, width - n)) for n in range(0, width, 512)]

    def scatter(left, weight, part, arrive, send_sems, recv_sems):
        copies = []
        for c, (start, size) in enumerate(columns):
            cols = pl.ds(start, size)
            part[:, cols] = jnp.dot(left, weight[:, cols], preferred_element_type=F32).astype(BF16)
            for n, (dz, dx) in enumerate(PEERS):
                src = part.at[pl.ds(slot_of(dz, dx) * tile, tile), cols]
                dst = arrive.at[pl.ds(slot_of(dz, -dx) * tile, tile), cols]
                copies.append(send(src, dst, send_sems.at[c, n], recv_sems.at[c, n], device(dz, dx)))
        return copies

    def collect(copies, part, arrive):
        for copy in copies:
            copy.wait()
        total = part[pl.ds(0, tile), :].astype(F32)
        for n in range(1, 8):
            total = total + arrive[pl.ds(n * tile, tile), :].astype(F32)
        return total

    scatter1 = scatter(ab[...], wo, p1, r1, r1_send, r1_recv)
    attention = collect(scatter1, p1, r1)
    middle = tok[...].astype(F32) + mod[2:3, :] * attention
    g2[pl.ds(0, tile), :] = modulate(middle, mod[3:4, :], mod[4:5, :])
    gather2 = spread(g2, g2_send, g2_recv)
    loads[8].wait()
    loads[9].wait()
    shared[4].wait()
    shared[5].wait()
    for copy in gather2:
        copy.wait()
    hidden = jax.nn.gelu(nt_dot(g2[...], wu[...]), approximate=True).astype(BF16)
    scatter2 = scatter(hidden, wd, p2, r2, r2_send, r2_recv)
    feed = collect(scatter2, p2, r2)
    leaving = middle + mod[5:6, :] * feed
    out_tok[...] = leaving.astype(BF16)
    final_input = modulate(leaving, mod[6:7, :], mod[7:8, :])
    loads[10].wait()
    loads[11].wait()
    vraw[...] = nt_dot(final_input, wf[...])
    pairs_of_tokens = tile // 2
    vx[...] = jnp.concatenate(
        [vraw[pl.ds(0, pairs_of_tokens, stride=2), :], vraw[pl.ds(1, pairs_of_tokens, stride=2), :]], axis=1
    )
    v_copy = send(vx, vr, v_send, v_recv, device(other_item=True))
    v_copy.wait()
    mine, theirs = vx[...], vr[...]
    is_guided = jnp.full(mine.shape, item % 2, jnp.int32) == 0
    guided = jnp.where(is_guided, mine, theirs)
    unguided = jnp.where(is_guided, theirs, mine)
    velocity = unguided + GUIDANCE * (guided - unguided)
    position = jnp.full(mine.shape, step_ref[0], jnp.int32).astype(F32)
    step_size = noise_level(position + 1.0) - noise_level(position)
    out_vel[...] = velocity
    out_lat[...] = lat[...] + step_size * velocity


def on_device(
    tokens,
    text_keys_values,
    text_length,
    modulation,
    input_weight,
    norm_gain,
    output_weight,
    up_weight,
    down_weight,
    final_weight,
    step_index,
    latent,
):
    tile = tokens.shape[1] * tokens.shape[2]
    width = tokens.shape[3]
    ff = up_weight.shape[1]
    half = 8 * tile
    chunks = -(-width // 512)
    operands = (
        text_length,
        step_index,
        tokens.reshape(tile, width),
        text_keys_values.reshape(-1, text_keys_values.shape[3]),
        modulation.reshape(8, width),
        input_weight.transpose(1, 0, 2),
        norm_gain,
        output_weight,
        up_weight.T,
        down_weight,
        final_weight.T,
        latent.reshape(-1, 128),
    )
    lat_shape = operands[-1].shape
    vmem = pltpu.VMEM
    dma = pltpu.SemaphoreType.DMA
    scratch = [
        vmem((tile, width), BF16),
        vmem(operands[3].shape, BF16),
        vmem((8, width), F32),
        vmem((width, 768), BF16),
        vmem(norm_gain.shape, F32),
        vmem((256, width), BF16),
        vmem((2 * ff, width), BF16),
        vmem((2 * ff, width), BF16),
        vmem((final_weight.shape[1], width), BF16),
        vmem(lat_shape, F32),
    ]
    scratch += [vmem((half, width), BF16)] * 6
    scratch += [
        vmem((4, 2, half, 256), BF16),
        vmem((half, 256), BF16),
        vmem((2 * half, 128), BF16),
        vmem((half, 128), BF16),
        vmem((half, 256), BF16),
        vmem((half, 128), BF16),
        vmem((4 * half, 128), F32),
        vmem((4 * half, 128), F32),
        vmem((4 * half, 128), F32),
        vmem((tile, final_weight.shape[1]), F32),
        vmem(lat_shape, F32),
        vmem(lat_shape, F32),
    ]
    scratch += [dma((12,)), dma((6,)), dma((6,)), dma((7,)), dma((7,)), dma((4, 2)), dma((4, 2))]
    scratch += [dma, dma, dma, dma, dma((chunks, 7)), dma((chunks, 7)), dma((7,)), dma((7,))]
    scratch += [dma((chunks, 7)), dma((chunks, 7)), dma, dma]
    smem = pl.BlockSpec(memory_space=pltpu.SMEM)
    hbm = pl.BlockSpec(memory_space=pl.ANY)
    whole = pl.BlockSpec(memory_space=pltpu.VMEM)
    tokens_out, velocity, latent_next = pl.pallas_call(
        layer_kernel,
        out_shape=(
            jax.ShapeDtypeStruct((tile, width), BF16),
            jax.ShapeDtypeStruct(lat_shape, F32),
            jax.ShapeDtypeStruct(lat_shape, F32),
        ),
        in_specs=[smem, smem] + [hbm] * 10,
        out_specs=(whole, whole, whole),
        scratch_shapes=scratch,
        compiler_params=pltpu.CompilerParams(
            collective_id=0, has_side_effects=True, vmem_limit_bytes=56 * 1024 * 1024
        ),
        name="layer",
    )(*operands)
    return (tokens_out.reshape(tokens.shape), velocity.reshape(latent.shape), latent_next.reshape(latent.shape))


def solution(mesh):
    in_specs = (
        P("item", "row", "col", None),
        P("item", None, None, "row"),
        P("item"),
        P("item", None, None),
        P(None, None, "row"),
        P(),
        P("row", None),
        P(None, "row"),
        P("row", None),
        P(),
        P(),
        P("item", "row", "col"),
    )
    out_specs = (P("item", "row", "col", None), P("item", "row", "col"), P("item", "row", "col"))
    return jax.shard_map(
        on_device, mesh=mesh, in_specs=in_specs, out_specs=out_specs, check_vma=False
    )
```

time: 312 us -> 76.5 us (0.25)
  waiting for transfers between devices: 225 us -> 0 us
  Pallas kernels: 0 us -> 68.2 us
  blocking collectives: 25.8 us -> 0 us
  matrix products: 18 us -> 0 us
  between operations: 15.4 us -> 1.93 us
  other arithmetic: 11.5 us -> 0 us
  local copies, waits for them, and re-layouts: 11.5 us -> 5.68 us
    psum x1 -> x0, waiting for transfers between devices: 124 us -> none  [on_device(): lax.psum(jnp.dot(attended, output_weight, preferred_element_type=jnp.floa...]
    pallas_call x0 -> x1, Pallas kernels: none -> 68.2 us  [on_device(): pl.pallas_call(layer_kernel, out_shape=(jax.ShapeDtypeStruct((tile, width...]
    reduce_scatter x1 -> x0, waiting for transfers between devices: 65.3 us -> none  [on_device(): lax.psum_scatter(jnp.dot(hidden, down_weight, preferred_element_type=jnp....]
    all_gather x1 -> x0, waiting for transfers between devices: 33.5 us -> none  [on_device(): stripe_tokens = lax.all_gather(tokens, 'row', axis=1, tiled=True)]
    all_gather x2 -> x0, blocking collectives: 25.8 us -> none  [the longest x1 13.2 us: on_device(): value_piece = lax.all_gather(values_image, 'col', axis=0, tiled=True)]
    dot_general x14 -> x0, matrix products: 18 us -> none  [the longest x1 7.51 us: on_device(): jnp.dot(hidden, down_weight, preferred_element_type=jnp.float32)]
    reduce_sum x13 -> x0, other arithmetic: 9.28 us -> none  [the longest x3 4.92 us: layer_norm(): center = values - jnp.mean(values, axis=-1, keepdims=True)]
  transfers between devices with their start and end apart: 4 -> 0, of which waited for: 4 -> 0; matrix products, arithmetic and copies ran while one was open for 2% -> 0% of each run, Pallas kernels for 0% -> 0%
where the time goes in v1:
time: 76.5 us; the launch traced here: 75.8 us
  Pallas kernels  68.2 us (89%)
  local copies, waits for them, and re-layouts  5.68 us (7%)
  between operations  1.93 us (3%)
    pallas_call x1, Pallas kernels, on_device(): pl.pallas_call(layer_kernel, out_shape=(jax.ShapeDtypeStruct((tile, width...  68.2 us
    unnamed x3, local copies, waits for them, and re-layouts  4.06 us
    reshape x1, local copies, waits for them, and re-layouts, on_device(): text_keys_values.reshape(-1, text_keys_values.shape[3])  1.62 us

profile of v1, /device:TPU:32, one launch (start us, length us, event | category | flops | bytes accessed | tf_op | source)
XLA Modules:
  0.0 75.8 jit_solution(8120329281028146941)
XLA Ops:
  1.9 1.6 %reshape.28.text_hbm = bf16[308,128]{1,0:T(8,128)(2,1)} reshape(bf16[1,154,2,128]{3,2,1,0:T(2,128)(2,1)} %param.13) | data formatting | bytes 157696 | tf_op jit(solution)/shard_map/reshape | solution.py:284
  3.5 68.2 %layer.1 = (bf16[16,2432]{1,0:T(8,128)(2,1)}, f32[8,128]{1,0:T(8,128)}, f32[8,128]{1,0:T(8,128)}) custom-call(s32[1]{0:T(128)S(6)} %copy.18.length_ref, s32[1]{0:T(128)S(6)} %copy.19.step_ref, bf16[16,2432]{1,0:T(8,128)(2,1)} %bitcast.12, bf16[308,128]{1,0:T(8,128)(2,1)} %reshape.28.text_hbm, f32[8,2432]{1,0:T(8,128)} %bitcast.13, ...), custom_call_target="tpu_custom_call" | custom-call | tf_op jit(solution)/shard_map/layer/pallas_call | solution.py:330
  71.7 1.5 %copy.20 = bf16[1,1,16,2432]{3,2,1,0:T(8,128)(2,1)} copy(bf16[1,1,16,2432]{3,2,1,0:T(8,128)(2,1)} %bitcast.14) | data formatting | bytes 155648
  73.3 1.3 %copy.21 = f32[1,1,1024]{2,1,0:T(1,128)} copy(f32[1,1,1024]{2,1,0:T(1,128)} %bitcast.17) | data formatting | bytes 8192
  74.5 1.3 %copy.22 = f32[1,1,1024]{2,1,0:T(1,128)} copy(f32[1,1,1024]{2,1,0:T(1,128)} %bitcast.16) | data formatting | bytes 8192

commit v2 on v1

--- a/solution.py
+++ b/solution.py
@@ -45,10 +45,10 @@
 
 
 def layer_kernel(
-    length_ref, step_ref, tok_hbm, text_hbm, mod_hbm, win_hbm, gain_hbm, wo_hbm, wu_hbm, wd_hbm, wf_hbm, lat_hbm,
-    out_tok, out_vel, out_lat,
-    tok, text, mod, wi, gain, wo, wu, wd, wf, lat,
-    g1, g2, p1, p2, r1, r2, kvr, kvs, qb, qs, ab, ats, s_max, s_sum, s_acc, vraw, vx, vr,
+    length_ref, tok_hbm, text_hbm, mod_hbm, win_hbm, gain_hbm, wo_hbm, wu_hbm, wd_hbm, wf_hbm,
+    out_tok, out_mine, out_theirs,
+    tok, text, mod, wi, gain, wo, wu, wd, wf,
+    g1, g2, p1, p2, r1, r2, kvr, kvs, qb, qs, ab, ats, s_max, s_sum, s_acc, vraw, vx, vr, text_keys, text_values,
     local_sem, w_send, w_recv, g1_send, g1_recv, kv_send, kv_recv, q_send, q_recv, a_send, a_recv,
     r1_send, r1_recv, g2_send, g2_recv, r2_send, r2_recv, v_send, v_recv,
 ):
@@ -75,7 +75,7 @@
     pairs = [(tok_hbm, tok), (mod_hbm, mod)]
     pairs += [(win_hbm.at[j], wi.at[:, pl.ds(128 * j, 128)]) for j in range(3)]
     pairs += [(text_hbm, text), (gain_hbm, gain), (wo_hbm, wo.at[pl.ds(0, 128)])]
-    pairs += [(wu_hbm, wu.at[pl.ds(0, ff)]), (wd_hbm, wd.at[pl.ds(0, ff)]), (wf_hbm, wf), (lat_hbm, lat)]
+    pairs += [(wu_hbm, wu.at[pl.ds(0, ff)]), (wd_hbm, wd.at[pl.ds(0, ff)]), (wf_hbm, wf)]
     loads = [pltpu.make_async_copy(src, dst, local_sem.at[j]) for j, (src, dst) in enumerate(pairs)]
     for load in loads:
         load.start()
@@ -92,17 +92,25 @@
     g1[pl.ds(0, tile), :] = modulate(states, mod[0:1, :], mod[1:2, :])
     pl.semaphore_wait(barrier, len(friends))
 
+    parts = [pl.ds(n, min(640, width - n)) for n in range(0, width, 640)]
+
     def spread(buf, send_sems, recv_sems):
         copies = []
-        for n, (dz, dx) in enumerate(PEERS):
-            to = slot_of(dz, -dx)
-            copies.append(
-                send(
-                    buf.at[pl.ds(0, tile)], buf.at[pl.ds(to * tile, tile)], send_sems.at[n], recv_sems.at[n],
-                    device(dz, dx),
-                )
-            )
+        for c, cols in enumerate(parts):
+            for n, (dz, dx) in enumerate(PEERS):
+                src = buf.at[pl.ds(0, tile), cols]
+                dst = buf.at[pl.ds(slot_of(dz, -dx) * tile, tile), cols]
+                copies.append(send(src, dst, send_sems.at[c, n], recv_sems.at[c, n], device(dz, dx)))
         return copies
+
+    def project(buf, copies, product):
+        total = None
+        for c, cols in enumerate(parts):
+            for copy in copies[7 * c : 7 * c + 7]:
+                copy.wait()
+            term = product(buf[:, cols], cols)
+            total = term if total is None else total + term
+        return total
 
     gather1 = spread(g1, g1_send, g1_recv)
     sibling = device(dk=1)
@@ -113,11 +121,10 @@
     loads[5].wait()
     loads[6].wait()
     text_rows = text.shape[0]
-    picked = lax.broadcasted_iota(jnp.int32, (TEXT_PAD, text_rows), 1)
-    wanted = 2 * lax.broadcasted_iota(jnp.int32, (TEXT_PAD, text_rows), 0)
-    text_all = text[...]
-    key_text = jnp.dot((picked == wanted).astype(BF16), text_all, preferred_element_type=F32).astype(BF16)
-    value_text = jnp.dot((picked == wanted + 1).astype(BF16), text_all, preferred_element_type=F32).astype(BF16)
+    text_keys[pl.ds(0, text_rows), :] = text[:, 0, :]
+    text_values[pl.ds(0, text_rows), :] = text[:, 1, :]
+    text_keys[pl.ds(text_rows, TEXT_PAD - text_rows), :] = jnp.zeros((TEXT_PAD - text_rows, 128), BF16)
+    text_values[pl.ds(text_rows, TEXT_PAD - text_rows), :] = jnp.zeros((TEXT_PAD - text_rows, 128), BF16)
     gains = gain[...]
     gain_rows = jnp.concatenate([gains, gains], axis=1)
     lane = lax.broadcasted_iota(jnp.int32, (1, 128), 1)
@@ -134,24 +141,24 @@
         loads[j].wait()
     for copy in shared[:3]:
         copy.wait()
-    for copy in gather1:
-        copy.wait()
-    projected = jnp.dot(g1[...], wi[...], preferred_element_type=F32)
+    projected = project(g1, gather1, lambda left, cols: jnp.dot(left, wi[cols, :], preferred_element_type=F32))
 
     kvs[:, 0:128] = root_norm(projected[:, 512:640], gain_rows[1:2]).astype(BF16)
     kvs[:, 128:256] = projected[:, 640:768].astype(BF16)
-    kvr[0, 0, :, 0:128] = root_norm(projected[:, 128:256], gain_rows[1:2]).astype(BF16)
-    kvr[0, 0, :, 128:256] = projected[:, 256:384].astype(BF16)
+    kvr[0, 0:half, 0:128] = root_norm(projected[:, 128:256], gain_rows[1:2]).astype(BF16)
+    kvr[0, 0:half, 128:256] = projected[:, 256:384].astype(BF16)
+    lower, upper = pl.ds(0, half), pl.ds(half, half)
     kv_copies = {}
-    for dc in (2, 1, 3):
-        kv_copies[4 - dc] = [
-            send(kvr.at[0, 0], kvr.at[4 - dc, 0], kv_send.at[dc, 0], kv_recv.at[4 - dc, 0], device(dc=dc)),
-            send(kvs, kvr.at[4 - dc, 1], kv_send.at[dc, 1], kv_recv.at[4 - dc, 1], device(dk=1, dc=dc)),
+    for dc in (1, 3, 2):
+        back = 4 - dc
+        kv_copies[back] = [
+            send(kvr.at[0, lower], kvr.at[back, lower], kv_send.at[dc, 0], kv_recv.at[back, 0], device(dc=dc)),
+            send(kvs, kvr.at[back, upper], kv_send.at[dc, 1], kv_recv.at[back, 1], device(dk=1, dc=dc)),
         ]
-    own_pair = send(kvs, kvr.at[0, 1], kv_send.at[0, 1], kv_recv.at[0, 1], sibling)
+    own_pair = send(kvs, kvr.at[0, upper], kv_send.at[0, 1], kv_recv.at[0, 1], sibling)
     qs[...] = (root_norm(projected[:, 384:512], gain_rows[0:1]) * HD ** (-0.5)).astype(BF16)
-    q_copy = send(qs, qb.at[pl.ds(half, half)], q_send, q_recv, sibling)
-    qb[pl.ds(0, half), :] = (root_norm(projected[:, 0:128], gain_rows[0:1]) * HD ** (-0.5)).astype(BF16)
+    q_copy = send(qs, qb.at[upper], q_send, q_recv, sibling)
+    qb[lower, :] = (root_norm(projected[:, 0:128], gain_rows[0:1]) * HD ** (-0.5)).astype(BF16)
 
     def attend(keys, values, chunks, keep=None):
         for n in chunks:
@@ -174,18 +181,17 @@
     s_sum[...] = jnp.zeros_like(s_sum)
     s_acc[...] = jnp.zeros_like(s_acc)
     keep = lax.broadcasted_iota(jnp.int32, (1, TEXT_PAD), 1) < length_ref[0]
-    attend(kvr[0, 0, :, 0:128], kvr[0, 0, :, 128:256], (0, 2))
-    attend(key_text, value_text, (0, 2), keep)
+    attend(text_keys[...], text_values[...], (0, 2), keep)
     q_copy.wait()
+    attend(text_keys[...], text_values[...], (1, 3), keep)
     own_pair.wait()
-    attend(kvr[0, 0, :, 0:128], kvr[0, 0, :, 128:256], (1, 3))
-    attend(key_text, value_text, (1, 3), keep)
-    attend(kvr[0, 1, :, 0:128], kvr[0, 1, :, 128:256], (1, 3, 0, 2))
-    for dc in (1, 3, 2):
+    attend(kvr[0, :, 0:128], kvr[0, :, 128:256], (1, 3, 0, 2))
+    for dc in (1, 3):
         for copy in kv_copies[dc]:
             copy.wait()
-        for part in range(2):
-            attend(kvr[dc, part, :, 0:128], kvr[dc, part, :, 128:256], (1, 3, 0, 2))
+        attend(kvr[dc, :, 0:128], kvr[dc, :, 128:256], (1, 3, 0, 2))
+    for copy in kv_copies[2]:
+        copy.wait()
 
     def attended(parity):
         low, high = pl.ds(parity * half, half), pl.ds((2 + parity) * half, half)
@@ -193,8 +199,10 @@
         second = s_acc[high, :] / s_sum[high, :]
         return jnp.where(lane < HD, first, second).astype(BF16)
 
+    attend(kvr[2, :, 0:128], kvr[2, :, 128:256], (1, 3))
     ats[...] = attended(1)
     a_copy = send(ats, ab.at[:, pl.ds(128, 128)], a_send, a_recv, sibling)
+    attend(kvr[2, :, 0:128], kvr[2, :, 128:256], (0, 2))
     ab[:, 0:128] = attended(0)
     loads[7].wait()
     shared[3].wait()
@@ -230,25 +238,28 @@
     loads[9].wait()
     shared[4].wait()
     shared[5].wait()
-    for copy in gather2:
-        copy.wait()
-    hidden = jax.nn.gelu(nt_dot(g2[...], wu[...]), approximate=True).astype(BF16)
+    up = project(g2, gather2, lambda left, cols: nt_dot(left, wu[:, cols]))
+    hidden = jax.nn.gelu(up, approximate=True).astype(BF16)
     scatter2 = scatter(hidden, wd, p2, r2, r2_send, r2_recv)
     feed = collect(scatter2, p2, r2)
     leaving = middle + mod[5:6, :] * feed
     out_tok[...] = leaving.astype(BF16)
     final_input = modulate(leaving, mod[6:7, :], mod[7:8, :])
     loads[10].wait()
-    loads[11].wait()
     vraw[...] = nt_dot(final_input, wf[...])
     pairs_of_tokens = tile // 2
     vx[...] = jnp.concatenate(
         [vraw[pl.ds(0, pairs_of_tokens, stride=2), :], vraw[pl.ds(1, pairs_of_tokens, stride=2), :]], axis=1
     )
     v_copy = send(vx, vr, v_send, v_recv, device(other_item=True))
+    out_mine[...] = vx[...]
     v_copy.wait()
-    mine, theirs = vx[...], vr[...]
-    is_guided = jnp.full(mine.shape, item % 2, jnp.int32) == 0
+    out_theirs[...] = vr[...]
+
+
+def guide_kernel(step_ref, tok, raw_mine, raw_theirs, lat, out_tok, out_vel, out_lat):
+    mine, theirs = raw_mine[...], raw_theirs[...]
+    is_guided = jnp.full(mine.shape, lax.axis_index("item") % 2, jnp.int32) == 0
     guided = jnp.where(is_guided, mine, theirs)
     unguided = jnp.where(is_guided, theirs, mine)
     velocity = unguided + GUIDANCE * (guided - unguided)
@@ -256,6 +267,7 @@
     step_size = noise_level(position + 1.0) - noise_level(position)
     out_vel[...] = velocity
     out_lat[...] = lat[...] + step_size * velocity
+    out_tok[...] = tok[...]
 
 
 def on_device(
@@ -279,9 +291,8 @@
     chunks = -(-width // 512)
     operands = (
         text_length,
-        step_index,
         tokens.reshape(tile, width),
-        text_keys_values.reshape(-1, text_keys_values.shape[3]),
+        text_keys_values.reshape(text_keys_values.shape[1:]),
         modulation.reshape(8, width),
         input_weight.transpose(1, 0, 2),
         norm_gain,
@@ -289,14 +300,14 @@
         up_weight.T,
         down_weight,
         final_weight.T,
-        latent.reshape(-1, 128),
-    )
-    lat_shape = operands[-1].shape
+    )
+    latent_rows = latent.reshape(-1, 128)
+    lat_shape = latent_rows.shape
     vmem = pltpu.VMEM
     dma = pltpu.SemaphoreType.DMA
     scratch = [
         vmem((tile, width), BF16),
-        vmem(operands[3].shape, BF16),
+        vmem(operands[2].shape, BF16),
         vmem((8, width), F32),
         vmem((width, 768), BF16),
         vmem(norm_gain.shape, F32),
@@ -304,11 +315,10 @@
         vmem((2 * ff, width), BF16),
         vmem((2 * ff, width), BF16),
         vmem((final_weight.shape[1], width), BF16),
-        vmem(lat_shape, F32),
     ]
     scratch += [vmem((half, width), BF16)] * 6
     scratch += [
-        vmem((4, 2, half, 256), BF16),
+        vmem((4, 2 * half, 256), BF16),
         vmem((half, 256), BF16),
         vmem((2 * half, 128), BF16),
         vmem((half, 128), BF16),
@@ -320,21 +330,24 @@
         vmem((tile, final_weight.shape[1]), F32),
         vmem(lat_shape, F32),
         vmem(lat_shape, F32),
+        vmem((TEXT_PAD, 128), BF16),
+        vmem((TEXT_PAD, 128), BF16),
     ]
-    scratch += [dma((12,)), dma((6,)), dma((6,)), dma((7,)), dma((7,)), dma((4, 2)), dma((4, 2))]
-    scratch += [dma, dma, dma, dma, dma((chunks, 7)), dma((chunks, 7)), dma((7,)), dma((7,))]
+    scratch += [dma((12,)), dma((6,)), dma((6,)), dma((4, 7)), dma((4, 7)), dma((4, 2)), dma((4, 2))]
+    scratch += [dma, dma, dma, dma, dma((chunks, 7)), dma((chunks, 7)), dma((4, 7)), dma((4, 7))]
     scratch += [dma((chunks, 7)), dma((chunks, 7)), dma, dma]
     smem = pl.BlockSpec(memory_space=pltpu.SMEM)
     hbm = pl.BlockSpec(memory_space=pl.ANY)
     whole = pl.BlockSpec(memory_space=pltpu.VMEM)
-    tokens_out, velocity, latent_next = pl.pallas_call(
+    outs = (
+        jax.ShapeDtypeStruct((tile, width), BF16),
+        jax.ShapeDtypeStruct(lat_shape, F32),
+        jax.ShapeDtypeStruct(lat_shape, F32),
+    )
+    leaving, mine, theirs = pl.pallas_call(
         layer_kernel,
-        out_shape=(
-            jax.ShapeDtypeStruct((tile, width), BF16),
-            jax.ShapeDtypeStruct(lat_shape, F32),
-            jax.ShapeDtypeStruct(lat_shape, F32),
-        ),
-        in_specs=[smem, smem] + [hbm] * 10,
+        out_shape=outs,
+        in_specs=[smem] + [hbm] * 9,
         out_specs=(whole, whole, whole),
         scratch_shapes=scratch,
         compiler_params=pltpu.CompilerParams(
@@ -342,6 +355,13 @@
         ),
         name="layer",
     )(*operands)
+    tokens_out, velocity, latent_next = pl.pallas_call(
+        guide_kernel,
+        out_shape=outs,
+        in_specs=[smem, whole, whole, whole, whole],
+        out_specs=(whole, whole, whole),
+        name="guide",
+    )(step_index, leaving, mine, theirs, latent_rows)
     return (tokens_out.reshape(tokens.shape), velocity.reshape(latent.shape), latent_next.reshape(latent.shape))
 
 

time: 76.5 us -> 63.2 us (0.83)
  Pallas kernels: 68.2 us -> 60.6 us
  local copies, waits for them, and re-layouts: 5.68 us -> 0 us
    pallas_call x1 -> x2, Pallas kernels: 68.2 us -> 60.6 us  [the longest x1 59.1 us: on_device(): pl.pallas_call(layer_kernel, out_shape=outs, in_specs=[smem] + [hbm] * 9,...]
    unnamed x3 -> x0, local copies, waits for them, and re-layouts: 4.06 us -> none
    reshape x1 -> x0, local copies, waits for them, and re-layouts: 1.62 us -> none  [on_device(): text_keys_values.reshape(-1, text_keys_values.shape[3])]
where the time goes in v2:
time: 63.2 us; the launch traced here: 62.6 us
  Pallas kernels  60.6 us (96%)
  between operations  1.93 us (3%)
    pallas_call x1, Pallas kernels, on_device(): pl.pallas_call(layer_kernel, out_shape=outs, in_specs=[smem] + [hbm] * 9,...  59.1 us
    pallas_call x1, Pallas kernels, on_device(): pl.pallas_call(guide_kernel, out_shape=outs, in_specs=[smem, whole, whole...  1.54 us

profile of v2, /device:TPU:32, one launch (start us, length us, event | category | flops | bytes accessed | tf_op | source)
XLA Modules:
  0.0 62.6 jit_solution(3919949195614107428)
XLA Ops:
  1.9 59.1 %layer.1 = (bf16[16,2432]{1,0:T(8,128)(2,1)}, f32[8,128]{1,0:T(8,128)}, f32[8,128]{1,0:T(8,128)}) custom-call(s32[1]{0:T(128)S(6)} %copy.15.length_ref, bf16[16,2432]{1,0:T(8,128)(2,1)} %bitcast.14, bf16[154,2,128]{2,1,0:T(2,128)(2,1)} %bitcast.13, f32[8,2432]{1,0:T(8,128)} %bitcast.15, bf16[3,2432,128]{2,1,0:T(8,128)(2,1)} %bitcast.11, f32[2,64]{1,0:T(2,128)} %gain_hbm.1, ...), custom_call_target="tpu_custom_call" | custom-call | tf_op jit(solution)/shard_map/layer/pallas_call | solution.py:347
  61.0 1.5 %guide.1 = (bf16[16,2432]{1,0:T(8,128)(2,1)}, f32[8,128]{1,0:T(8,128)}, f32[8,128]{1,0:T(8,128)}) custom-call(s32[1]{0:T(128)S(6)} %copy.16.step_ref, bf16[16,2432]{1,0:T(8,128)(2,1)} %get-tuple-element.9.tok, f32[8,128]{1,0:T(8,128)} %get-tuple-element.10.raw_mine, f32[8,128]{1,0:T(8,128)} %get-tuple-element.11.raw_theirs, f32[8,128]{1,0:T(8,128)} %bitcast.16), custom_call_target="tpu_custom_call" | custom-call | tf_op jit(solution)/shard_map/guide/pallas_call | solution.py:358
